TPU v7x, 32 devices: a whole 2x2x4 slice. The times are simulated.
32 devices in a mesh: dp: 8 (over z, y), seq: 4 (over x, core).
Axes of the slice: x: 2, y: 2, z: 4, core: 2. Of those that a mesh axis runs over, the one named last changes fastest.
Arguments:
- hidden_states: bfloat16 [4096, 2048], P(('dp', 'seq'))
- query_weight: bfloat16 [2048, 512], P('dp')
- key_weight: bfloat16 [2048, 128], P('dp')
- value_weight: bfloat16 [2048, 128], P('dp'), may hold values from -0.125 to 0.125
- doc_lengths: int32 [8, 8], P('dp'), may hold values from 1 to 256, 512 in all within a row
Outputs:
- context: bfloat16 [4096, 512], P(('dp', 'seq'))
Inputs may be any that keep to these rules, and one draw needn't show every extreme that they name: `doc_lengths`: each row sums to 512, and its longest document has exactly 256 tokens.
All inputs are finite; a program needn't handle non-finite values.
Results may differ from a plain program's by a relative error of at most 0.0076.
Values may be sent and summed in bfloat16 or wider, within the bound.
A program may use at most 64 MiB of HBM per device.

v0:
```python
import math

import jax
import jax.numpy as jnp
from jax import lax
from jax.sharding import PartitionSpec as P

HD = 64


EPSILON = 1e-05
THETA = 500000.0
NEG_FILL = -1e30


def normalize(states):
    floats = states.astype(jnp.float32)
    scale = lax.rsqrt(jnp.mean(floats * floats, axis=-1, keepdims=True) + EPSILON)
    return (floats * scale).astype(jnp.bfloat16)


def doc_offsets(doc_sizes, positions):
    ends = jnp.cumsum(doc_sizes)
    before = (ends[None, :] <= positions[:, None]).astype(jnp.int32)
    docs = jnp.sum(before, axis=1)
    starts = jnp.sum(before * doc_sizes[None, :], axis=1)
    return (docs, positions - starts)


def rotate(vectors, offset):
    half_dim = vectors.shape[-1] // 2
    index = jnp.arange(half_dim, dtype=jnp.float32)
    freqs = jnp.exp(index * (-2.0 / vectors.shape[-1]) * math.log(THETA))
    angle = offset.astype(jnp.float32)[:, None] * freqs[None, :]
    cosine = jnp.cos(angle)[:, None, :]
    sine = jnp.sin(angle)[:, None, :]
    first = vectors[..., :half_dim]
    second = vectors[..., half_dim:]
    return jnp.concatenate(
        [first * cosine - second * sine, second * cosine + first * sine], axis=-1
    )


def attend(queries, keys, values, docs):
    seq_length = queries.shape[0]
    group = queries.shape[1]
    scale = queries.shape[-1] ** (-0.5)
    block = math.gcd(256, seq_length)
    key_pos = jnp.arange(seq_length, dtype=jnp.int32)

    def one_block(number):
        first_row = number * block
        query_block = lax.dynamic_slice_in_dim(queries, first_row, block, 0)
        query_docs = lax.dynamic_slice_in_dim(docs, first_row, block, 0)
        query_pos = first_row + jnp.arange(block, dtype=jnp.int32)
        scores = (
            jnp.einsum("qgd,kd->gqk", query_block, keys, preferred_element_type=jnp.float32) * scale
        )
        allowed = (key_pos[None, :] <= query_pos[:, None]) & (docs[None, :] == query_docs[:, None])
        scores = jnp.where(allowed[None], scores, NEG_FILL)
        highest = jnp.max(scores, axis=-1, keepdims=True)
        expons = jnp.exp(scores - highest)
        totals = jnp.sum(expons, axis=-1, keepdims=True)
        weights = (expons / totals).astype(jnp.bfloat16)
        mixed = jnp.einsum("gqk,kd->qgd", weights, values, preferred_element_type=jnp.float32)
        return mixed.astype(jnp.bfloat16)

    blocks = lax.map(one_block, jnp.arange(seq_length // block, dtype=jnp.int32))
    return blocks.reshape(seq_length, group * queries.shape[-1])


def shards(hidden_states, query_weight, key_weight, value_weight, doc_lengths):
    tok_count = hidden_states.shape[0]
    seq_count = lax.axis_size("seq")
    seq_index = lax.axis_index("seq")
    seq_length = tok_count * seq_count
    head_dim = HD
    heads_here = query_weight.shape[1] // (head_dim * seq_count)
    kv_heads = key_weight.shape[1] // head_dim
    normed = normalize(hidden_states)
    doc_sizes = doc_lengths[0]
    all_positions = jnp.arange(seq_length, dtype=jnp.int32)
    docs_all, offset_all = doc_offsets(doc_sizes, all_positions)
    pieces = (
        lax.all_gather(query_weight, "dp", axis=0, tiled=True),
        lax.all_gather(key_weight, "dp", axis=0, tiled=True),
        lax.all_gather(value_weight, "dp", axis=0, tiled=True),
    )
    query_lin, key_lin, value_lin = tuple(
        (jnp.dot(normed, piece, preferred_element_type=jnp.float32) for piece in pieces)
    )
    own_offset = lax.dynamic_slice_in_dim(offset_all, seq_index * tok_count, tok_count, 0)
    query_rot = (
        rotate(query_lin.reshape(tok_count, -1, head_dim), own_offset)
        .astype(jnp.bfloat16)
        .reshape(tok_count, -1)
    )
    key_rot = rotate(key_lin.reshape(tok_count, kv_heads, head_dim), own_offset).astype(
        jnp.bfloat16
    )
    value_cast = value_lin.astype(jnp.bfloat16).reshape(tok_count, kv_heads, head_dim)
    key_value = jnp.concatenate([key_rot, value_cast], axis=2)
    repeated = jnp.repeat(key_value, seq_count // kv_heads, axis=1).reshape(tok_count, -1)
    query_heads, kv_local = (
        lax.all_to_all(query_rot, "seq", split_axis=1, concat_axis=0, tiled=True),
        lax.all_to_all(repeated, "seq", split_axis=1, concat_axis=0, tiled=True),
    )
    key_local = kv_local[:, :head_dim]
    value_local = kv_local[:, head_dim:]
    mixed_heads = attend(
        query_heads.reshape(seq_length, heads_here, head_dim), key_local, value_local, docs_all
    )
    return lax.all_to_all(mixed_heads, "seq", split_axis=0, concat_axis=1, tiled=True)


def solution(mesh):
    placed = (P(("dp", "seq"), None), P("dp", None), P("dp", None), P("dp", None), P("dp", None))
    return jax.shard_map(
        shards, mesh=mesh, in_specs=placed, out_specs=P(("dp", "seq"), None), check_vma=False
    )
```

profile of v0, /device:TPU:0, one launch (start us, length us, event | category | flops | bytes accessed | tf_op | source)
XLA Modules:
  0.0 120.7 jit_solution(3050384695510439155)
XLA Ops:
  6.5 0.0 copy-start
  6.5 0.0 copy-start.1
  6.5 0.0 all-gather.2.cloned.1.call-start
  6.5 0.7 all-gather.2.cloned.1.call-update
  7.3 0.8 reduce-window.8
  8.1 0.7 select_reduce_fusion
  8.9 0.1 dynamic-slice_convert_fusion
  8.9 1.2 %fusion.23 = f32[128]{0:T(128)S(1)} fusion(bf16[128,2048]{1,0:T(8,128)(2,1)} %param.7), kind=kLoop, calls=%fused_computation.27 | loop fusion | flops 786304 | bytes 524800 | tf_op jit(solution)/shard_map/reduce_sum | solution.py:18
  10.2 0.1 multiply_cosine_fusion
  10.3 34.1 %all_gather.10 = bf16[2048,128]{1,0:T(8,128)(2,1)S(1)} all-gather(bf16[256,128]{1,0:T(8,128)(2,1)} %param.9), channel_id=1, replica_groups=mesh['dp'=8,'seq'=4] {'dp'}, dimensions={0}, use_global_device_ids=true | all-gather | bytes 589824 | tf_op jit(solution)/shard_map/all_gather | solution.py:86
  44.5 1.4 %fusion.26 = f32[128,128]{0,1:T(8,128)S(1)} fusion(bf16[2048,128]{1,0:T(8,128)(2,1)S(1)} %all_gather.10, bf16[128,2048]{1,0:T(8,128)(2,1)} %param.7, f32[128]{0:T(128)S(1)} %add_rsqrt_fusion), kind=kOutput, calls=%fused_computation.44 | convolution fusion | flops 67895296 | bytes 1114624 | tf_op jit(solution)/shard_map/dot_general | solution.py:90
  45.9 0.0 copy-done.1
  45.9 32.3 %all_gather.11 = bf16[2048,128]{1,0:T(8,128)(2,1)S(1)} all-gather(bf16[256,128]{1,0:T(8,128)(2,1)S(1)} %copy-done.1), channel_id=1, replica_groups=mesh['dp'=8,'seq'=4] {'dp'}, dimensions={0}, use_global_device_ids=true | all-gather | bytes 589824 | tf_op jit(solution)/shard_map/all_gather | solution.py:87
  78.2 0.0 copy-done
  78.2 0.4 convolution_convert_fusion.1
  78.7 0.7 broadcast_in_dim.16
  79.3 3.3 %all-to-all-start.1 = ((bf16[128,4,128]{0,2,1:T(8,128)(2,1)}), bf16[128,4,128]{0,2,1:T(8,128)(2,1)S(1)}, u32[]{:S(2)}, u32[]{:S(2)}) async-start(bf16[128,4,128]{0,2,1:T(8,128)(2,1)} %bitcast.8), calls=%async_computation.1 | async-start | bytes 262144 | tf_op jit(solution)/shard_map/all_to_all | solution.py:106
  82.7 4.6 %all-to-all-done.1 = bf16[128,4,128]{0,2,1:T(8,128)(2,1)S(1)} async-done(((bf16[128,4,128]{0,2,1:T(8,128)(2,1)}), bf16[128,4,128]{0,2,1:T(8,128)(2,1)S(1)}, u32[]{:S(2)}, u32[]{:S(2)}) %all-to-all-start.1) | async-done | bytes 131104 | tf_op jit(solution)/shard_map/all_to_all | solution.py:106
  87.2 0.1 copy.34
  87.4 0.0 all-gather.2.cloned.1.call-done
  87.4 2.6 %fusion.28 = f32[128,512]{0,1:T(8,128)S(1)} fusion(bf16[2048,512]{1,0:T(8,128)(2,1)} %all-gather.2.cloned.1.call-done, bf16[128,2048]{1,0:T(8,128)(2,1)S(1)} %copy-done, f32[128]{0:T(128)S(1)} %add_rsqrt_fusion), kind=kOutput, calls=%fused_computation.45 | convolution fusion | flops 269221888 | bytes 2884096 | tf_op jit(solution)/shard_map/dot_general | solution.py:90
  90.0 0.7 pad_maximum_fusion
  90.7 3.3 %all-to-all-start = ((bf16[128,4,128]{0,2,1:T(8,128)(2,1)}), bf16[128,4,128]{0,2,1:T(8,128)(2,1)S(1)}, u32[]{:S(2)}, u32[]{:S(2)}) async-start(bf16[128,4,128]{0,2,1:T(8,128)(2,1)} %bitcast.4), calls=%async_computation | async-start | bytes 262144 | tf_op jit(solution)/shard_map/all_to_all | solution.py:105
  94.0 0.1 fusion.35
  94.1 0.1 copy.36
  94.2 0.1 copy.35
  94.3 4.2 %all-to-all-done = bf16[128,4,128]{0,2,1:T(8,128)(2,1)S(1)} async-done(((bf16[128,4,128]{0,2,1:T(8,128)(2,1)}), bf16[128,4,128]{0,2,1:T(8,128)(2,1)S(1)}, u32[]{:S(2)}, u32[]{:S(2)}) %all-to-all-start) | async-done | bytes 131104 | tf_op jit(solution)/shard_map/all_to_all | solution.py:105
  98.6 0.1 copy.33
  98.7 0.1 reshape.178
  98.7 7.1 %while.11 = (s32[]{:T(128)}, bf16[2,256,2,64]{1,3,2,0:T(8,128)(2,1)S(1)}, s32[2]{0:T(128)S(1)}, s32[512]{0:T(512)S(1)}, bf16[512,2,64]{0,2,1:T(8,128)(2,1)S(1)},...) while((s32[]{:T(128)}, ...), condition=%wide.region_7.8_spmd.clone, body=%wide.region_4.7_spmd.clone.sunk | while | flops 103450368 | bytes 3943619 | solution.py:68
  98.8 0.6 dynamic_slice.31
  100.0 0.1 dynamic_slice.32
  100.1 0.2 fusion.56
  100.3 0.6 fusion.57
  100.9 0.3 fusion.58
  101.2 1.1 fusion.59
  102.3 0.6 dynamic_slice.31
  103.6 0.1 dynamic_slice.32
  103.7 0.2 fusion.56
  103.8 0.6 fusion.57
  104.4 0.3 fusion.58
  104.8 1.1 fusion.59
  105.9 0.1 copy.37
  106.0 0.1 all_to_all.44
  106.1 7.0 %all_to_all.51 = bf16[4,128,128]{1,2,0:T(8,128)(2,1)S(1)} all-to-all(bf16[4,128,128]{1,2,0:T(8,128)(2,1)S(1)} %copy.38), channel_id=1, replica_groups=mesh['dp'=8,'seq'=4] {'seq'}, dimensions={0} | all-to-all | bytes 262144 | tf_op jit(solution)/shard_map/all_to_all | solution.py:113
  113.1 0.8 copy.39
  (11 shorter events, 0.1 us)
Async XLA Ops:
  6.5 71.7 %copy-start = (bf16[128,2048]{1,0:T(8,128)(2,1)S(1)}, bf16[128,2048]{1,0:T(8,128)(2,1)}, u32[]{:S(2)}) copy-start(bf16[128,2048]{1,0:T(8,128)(2,1)} %param.7) | copy-start | bytes 1572868
  6.5 39.4 %copy-start.1 = (bf16[256,128]{1,0:T(8,128)(2,1)S(1)}, bf16[256,128]{1,0:T(8,128)(2,1)}, u32[]{:S(2)}) copy-start(bf16[256,128]{1,0:T(8,128)(2,1)} %param.10) | copy-start | bytes 196612
  6.5 80.8 %all-gather.2.cloned.1.call-start = ((), (), s32[]{:S(2)}) async-start(), calls=%async_computation.3 | async-start | bytes 2359296 | tf_op jit(solution)/shard_map/all_gather | solution.py:85
  79.3 7.9 %all-to-all-start.1 = ((bf16[128,4,128]{0,2,1:T(8,128)(2,1)}), bf16[128,4,128]{0,2,1:T(8,128)(2,1)S(1)}, u32[]{:S(2)}, u32[]{:S(2)}) async-start(bf16[128,4,128]{0,2,1:T(8,128)(2,1)} %bitcast.8), calls=%async_computation.1 | async-start | bytes 262144 | tf_op jit(solution)/shard_map/all_to_all | solution.py:106
  90.7 7.9 %all-to-all-start = ((bf16[128,4,128]{0,2,1:T(8,128)(2,1)}), bf16[128,4,128]{0,2,1:T(8,128)(2,1)S(1)}, u32[]{:S(2)}, u32[]{:S(2)}) async-start(bf16[128,4,128]{0,2,1:T(8,128)(2,1)} %bitcast.4), calls=%async_computation | async-start | bytes 262144 | tf_op jit(solution)/shard_map/all_to_all | solution.py:105
Sparse Core Ops, SparseCore 0:
  9.5 57.2 all-gather.1
where the time goes:
time: 121 us
  blocking collectives  73.4 us (61%)
  between operations  13.6 us (11%)
  waiting for transfers between devices  9.54 us (8%)
  matrix products  8.37 us (7%)
  starting transfers between devices  6.65 us (5%)
  other arithmetic  4.16 us (3%)
  local copies, waits for them, and re-layouts  3.63 us (3%)
  loops' own time  1.41 us (1%)
    all_gather x1, blocking collectives, shards(): lax.all_gather(key_weight, 'dp', axis=0, tiled=True)  34.1 us
    all_gather x1, blocking collectives, shards(): lax.all_gather(value_weight, 'dp', axis=0, tiled=True)  32.3 us
    all_to_all x1, blocking collectives, shards(): lax.all_to_all(mixed_heads, 'seq', split_axis=0, concat_axis=1, tiled=True)  6.99 us
    all_to_all x1, waiting for transfers between devices, shards(): lax.all_to_all(repeated, 'seq', split_axis=1, concat_axis=0, tiled=True)  4.56 us
    dot_general x3, matrix products, shards(): jnp.dot(normed, piece, preferred_element_type=jnp.float32)  4.36 us
    all_to_all x1, waiting for transfers between devices, shards(): lax.all_to_all(query_rot, 'seq', split_axis=1, concat_axis=0, tiled=True)  4.25 us
    all_to_all x1, starting transfers between devices, shards(): lax.all_to_all(repeated, 'seq', split_axis=1, concat_axis=0, tiled=True)  3.33 us
    all_to_all x1, starting transfers between devices, shards(): lax.all_to_all(query_rot, 'seq', split_axis=1, concat_axis=0, tiled=True)  3.33 us
  transfers between devices with their start and end apart: 3, of which 2 were waited for; matrix products, arithmetic and copies ran while one was open for 5% of the time, Pallas kernels for 0%

commit v1 on v0

v1 whole, which is shorter than its diff:
```python
import functools
import math

import jax
import jax.numpy as jnp
from jax import lax
from jax.experimental import pallas as pl
from jax.experimental.pallas import tpu as pltpu
from jax.sharding import PartitionSpec as P

HD = 64
GROUP = 4
LANES = 128
INNER = 2
CORES = 2
PIECES = 4
EPSILON = 1e-05
THETA = 500000.0
NEG_FILL = -1e30
MESH = pl.DeviceIdType.MESH


def kernel(n_dp, n_seq, docs, h_ref, q_ref, k_ref, v_ref, len_ref, out_ref,
           hid, nrm, wbuf, kraw, vraw, cos_buf, sin_buf, bias, qs, ks, v0, v1, ctx,
           loc_sem, hs_sem, hf_sem, hc_sem, hr_sem, ws_sem, wr_sem, os_sem, or_sem):
    dp = lax.axis_index("dp")
    me = lax.axis_index("seq")
    tok, depth = h_ref.shape
    kd = q_ref.shape[0]
    length = tok * n_seq
    n_z = n_dp // INNER
    n_x = n_seq // CORES
    z, y = dp // INNER, dp % INNER
    x, core = me // CORES, me % CORES
    mate = x * CORES + (1 - core)
    rows = tok // PIECES
    kv_head = (me * (LANES // HD)) // GROUP
    kv_block = pl.multiple_of((kv_head * HD // LANES) * LANES, LANES)
    kv_odd = (kv_head * HD // LANES) * LANES != kv_head * HD
    window = length // 2

    def dev(d, s):
        return {"dp": d, "seq": s}

    def own_rows(index):
        return pl.ds(pl.multiple_of(index * kd, kd), kd)

    q_cols = pl.ds(pl.multiple_of(me * LANES, LANES), LANES)
    local = [
        pltpu.make_async_copy(k_ref.at[:, pl.ds(kv_block, LANES)], kraw, loc_sem.at[0]),
        pltpu.make_async_copy(v_ref.at[:, pl.ds(kv_block, LANES)], vraw, loc_sem.at[1]),
        pltpu.make_async_copy(q_ref.at[:, q_cols], wbuf.at[own_rows(dp), pl.ds(0, LANES)], loc_sem.at[2]),
        pltpu.make_async_copy(h_ref, hid.at[me], loc_sem.at[3]),
    ]
    for copy in local:
        copy.start()

    has_left, has_right = z > 0, z < n_z - 1
    left, right, across = dp - INNER, dp + INNER, z * INNER + (1 - y)

    barrier = pltpu.get_barrier_semaphore()
    for step in range(1, n_seq):
        pl.semaphore_signal(barrier, inc=1, device_id=dev(dp, (me + step) % n_seq), device_id_type=MESH)
    pl.semaphore_signal(barrier, inc=1, device_id=dev(across, me), device_id_type=MESH)

    @pl.when(has_left)
    def _():
        pl.semaphore_signal(barrier, inc=1, device_id=dev(left, me), device_id_type=MESH)

    @pl.when(has_right)
    def _():
        pl.semaphore_signal(barrier, inc=1, device_id=dev(right, me), device_id_type=MESH)

    pl.semaphore_wait(barrier, n_seq + has_left.astype(jnp.int32) + has_right.astype(jnp.int32))

    def piece_rows(piece):
        return pl.ds(piece * rows, rows)

    def h_copy(src, source, piece, send_sem, target):
        return pltpu.make_async_remote_copy(
            src_ref=src,
            dst_ref=hid.at[source, piece_rows(piece)],
            send_sem=send_sem,
            recv_sem=hr_sem.at[source, piece],
            device_id=dev(dp, target),
            device_id_type=MESH,
        )

    def h_to_x(step, piece):
        target = ((x + step) % n_x) * CORES + core
        return h_copy(h_ref.at[piece_rows(piece)], me, piece, hs_sem.at[step, piece], target)

    def h_to_mate(piece):
        return h_copy(h_ref.at[piece_rows(piece)], me, piece, hc_sem.at[piece], mate)

    def h_forward(step, piece):
        source = ((x + n_x - step) % n_x) * CORES + core
        return h_copy(hid.at[source, piece_rows(piece)], source, piece, hf_sem.at[step, piece], mate)

    def w_copy(shard, part, way, target, src=None):
        place = wbuf.at[own_rows(shard), pl.ds(part * LANES, LANES)]
        return pltpu.make_async_remote_copy(
            src_ref=place if src is None else src,
            dst_ref=place,
            send_sem=ws_sem.at[way, shard, part],
            recv_sem=wr_sem.at[shard, part],
            device_id=dev(target, me),
            device_id_type=MESH,
        )

    def w_own(part, way, target):
        return w_copy(dp, part, way, target, q_ref.at[:, q_cols] if part == 0 else None)

    def send_own(part, act):
        @pl.when(has_left)
        def _():
            act(w_own(part, 0, left))

        @pl.when(has_right)
        def _():
            act(w_own(part, 1, right))

        act(w_own(part, 2, across))

    start = lambda copy: copy.start()
    wait_send = lambda copy: copy.wait_send()

    for step in range(1, n_x):
        h_to_x(step, 0).start()
    send_own(0, start)
    for piece in range(1, PIECES):
        for step in range(1, n_x):
            h_to_x(step, piece).start()
    for piece in range(PIECES):
        h_to_mate(piece).start()

    local[0].wait()
    local[1].wait()
    lane_k = lax.broadcasted_iota(jnp.int32, (kd, LANES), 1)
    kw = kraw[...].astype(jnp.float32)
    vw = vraw[...].astype(jnp.float32)
    first = jnp.where(kv_odd, pltpu.roll(kw, HD, 1), kw)
    second = jnp.where(kv_odd, vw, pltpu.roll(vw, HD, 1))
    wbuf[own_rows(dp), LANES:] = jnp.where(lane_k < HD, first, second).astype(wbuf.dtype)
    local[2].wait()
    send_own(1, start)

    half = HD // 2
    ends = [len_ref[0, 0]]
    for j in range(1, docs):
        ends.append(ends[-1] + len_ref[0, j])
    lane = lax.broadcasted_iota(jnp.int32, (tok, LANES), 1)
    row = lax.broadcasted_iota(jnp.int32, (tok, LANES), 0)
    freqs = jnp.exp((lane % half).astype(jnp.float32) * (-2.0 / HD) * math.log(THETA))

    def key_range(block):
        low = max(0, block * tok - window)
        return low - low % tok, (block + 1) * tok

    def tables(block):
        pos = row + block * tok
        begin = jnp.zeros((tok, LANES), jnp.int32)
        for j in range(docs):
            begin = jnp.where(ends[j] <= pos, ends[j], begin)
        angle = (pos - begin).astype(jnp.float32) * freqs
        cos_buf[block * tok:(block + 1) * tok] = jnp.cos(angle)
        sine = jnp.sin(angle)
        sin_buf[block * tok:(block + 1) * tok] = jnp.where(lane % HD < half, -sine, sine)
        low, high = key_range(block)
        for number, base in enumerate(range(low, high, LANES)):
            key = lane + base
            fine = (key >= begin) & (key <= pos)
            bias[block, :, number * LANES:(number + 1) * LANES] = jnp.where(fine, 1.0, 0.0)

    def normalize(source, piece):
        floats = hid[source, piece_rows(piece)].astype(jnp.float32)
        scale = lax.rsqrt(jnp.mean(floats * floats, axis=-1, keepdims=True) + EPSILON)
        place = pl.ds(pl.multiple_of(source * tok, tok) + piece * rows, rows)
        nrm[place] = (floats * scale).astype(nrm.dtype)

    def relay_h(piece):
        for step in range(1, n_x):
            copy = h_forward(step, piece)
            copy.wait_recv()
            copy.start()
        for step in range(1, n_x):
            normalize(((x + n_x - step) % n_x) * CORES + core, piece)

    def relay_w(d):
        for part in range(2):
            @pl.when(z >= d)
            def _():
                shard = dp - d * INNER
                w_copy(shard, part, 1, dp).wait_recv()

                @pl.when(has_right)
                def _():
                    w_copy(shard, part, 1, right).start()

                w_copy(shard, part, 2, across).start()

            @pl.when(z + d < n_z)
            def _():
                shard = dp + d * INNER
                w_copy(shard, part, 0, dp).wait_recv()

                @pl.when(has_left)
                def _():
                    w_copy(shard, part, 0, left).start()

                w_copy(shard, part, 2, across).start()

    def mate_h(source, piece):
        h_copy(hid.at[source, piece_rows(piece)], source, piece, hc_sem.at[piece], mate).wait_recv()
        normalize(source, piece)

    local[3].wait()
    for piece in range(PIECES):
        normalize(me, piece)
    for piece in range(PIECES):
        mate_h(mate, piece)

    n_table = 0
    for turn in range(max(PIECES, n_z - 1)):
        if n_table < n_seq:
            tables(n_table)
            n_table += 1
        if turn < PIECES:
            relay_h(turn)
        if turn + 1 < n_z:
            relay_w(turn + 1)
    for block in range(n_table, n_seq):
        tables(block)

    for outer in range(n_z):
        shard = outer * INNER + (1 - y)
        for part in range(2):
            w_copy(shard, part, 2, across).wait_recv()
    for piece in range(PIECES):
        for step in range(1, n_x):
            mate_h(((x + n_x - step) % n_x) * CORES + (1 - core), piece)

    strip = math.gcd(length, 512)
    lane_s = lax.broadcasted_iota(jnp.int32, (strip, LANES), 1)
    low_half = lane_s % HD < half
    low_head = lane_s < HD
    for base in range(0, length, strip):
        place = slice(base, base + strip)
        lin = jnp.dot(nrm[place], wbuf[...], preferred_element_type=jnp.float32)
        cosine, sine = cos_buf[place], sin_buf[place]

        def rotate(part):
            other = jnp.where(low_half, pltpu.roll(part, LANES - half, 1), pltpu.roll(part, half, 1))
            return part * cosine + other * sine

        query, kv = lin[:, :LANES], lin[:, LANES:]
        query = rotate(query) * HD ** -0.5
        qs[0, place] = jnp.where(low_head, query, 0.0).astype(qs.dtype)
        qs[1, place] = jnp.where(low_head, 0.0, query).astype(qs.dtype)
        key = rotate(kv)
        ks[place] = jnp.where(low_head, key, pltpu.roll(key, HD, 1)).astype(ks.dtype)
        v0[place] = jnp.where(low_head, pltpu.roll(kv, HD, 1), 1.0).astype(v0.dtype)
        v1[place] = jnp.where(low_head, 1.0, kv).astype(v1.dtype)

    def o_copy(block):
        return pltpu.make_async_remote_copy(
            src_ref=ctx.at[block],
            dst_ref=out_ref.at[:, q_cols],
            send_sem=os_sem.at[block],
            recv_sem=or_sem.at[me],
            device_id=dev(dp, block),
            device_id_type=MESH,
        )

    low_tok = lax.broadcasted_iota(jnp.int32, (tok, LANES), 1) < HD
    for block in reversed(range(n_seq)):
        low, high = key_range(block)
        place = slice(block * tok, (block + 1) * tok)
        allowed = bias[block, :, :high - low] > 0.5
        outs = []
        for head, values in ((0, v0), (1, v1)):
            scores = lax.dot_general(
                qs[head, place], ks[low:high], (((1,), (1,)), ((), ())),
                preferred_element_type=jnp.float32,
            )
            scores = jnp.where(allowed, scores, NEG_FILL)
            highest = jnp.max(scores, axis=-1, keepdims=True)
            expons = jnp.exp(scores - highest).astype(values.dtype)
            outs.append(jnp.dot(expons, values[low:high], preferred_element_type=jnp.float32))
        mixed = jnp.where(low_tok, outs[0], outs[1])
        totals = pltpu.roll(jnp.where(low_tok, outs[1], outs[0]), HD, 1)
        ctx[block] = (mixed / totals).astype(ctx.dtype)

        @pl.when(me != block)
        def _():
            o_copy(block).start()

        @pl.when(me == block)
        def _():
            out_ref[:, q_cols] = ctx[block]

    for step in range(1, n_seq):
        source = (me + step) % n_seq
        cols = pl.ds(pl.multiple_of(source * LANES, LANES), LANES)
        pltpu.make_async_remote_copy(
            src_ref=ctx.at[0], dst_ref=out_ref.at[:, cols], send_sem=os_sem.at[0],
            recv_sem=or_sem.at[source], device_id=dev(dp, source), device_id_type=MESH,
        ).wait_recv()

    for block in range(n_seq):
        @pl.when(me != block)
        def _():
            o_copy(block).wait_send()
    for piece in range(PIECES):
        h_to_mate(piece).wait_send()
        for step in range(1, n_x):
            h_to_x(step, piece).wait_send()
            h_forward(step, piece).wait_send()
    for part in range(2):
        send_own(part, wait_send)
        for d in range(1, n_z):
            @pl.when(z >= d)
            def _():
                @pl.when(has_right)
                def _():
                    w_copy(dp - d * INNER, part, 1, right).wait_send()

                w_copy(dp - d * INNER, part, 2, across).wait_send()

            @pl.when(z + d < n_z)
            def _():
                @pl.when(has_left)
                def _():
                    w_copy(dp + d * INNER, part, 0, left).wait_send()

                w_copy(dp + d * INNER, part, 2, across).wait_send()


def shards(hidden_states, query_weight, key_weight, value_weight, doc_lengths):
    n_dp, n_seq = lax.axis_size("dp"), lax.axis_size("seq")
    tok, depth = hidden_states.shape
    kd = query_weight.shape[0]
    length = tok * n_seq
    docs = doc_lengths.shape[1]
    span = min(length, length // 2 + tok)
    half_type, full = jnp.bfloat16, jnp.float32
    any_spec = pl.BlockSpec(memory_space=pl.ANY)
    dma = pltpu.SemaphoreType.DMA
    n_x = n_seq // CORES
    return pl.pallas_call(
        functools.partial(kernel, n_dp, n_seq, docs),
        out_shape=jax.ShapeDtypeStruct((tok, query_weight.shape[1]), half_type),
        in_specs=[any_spec] * 4 + [pl.BlockSpec(memory_space=pltpu.SMEM)],
        out_specs=pl.BlockSpec(memory_space=pltpu.VMEM),
        scratch_shapes=[
            pltpu.VMEM((n_seq, tok, depth), half_type),
            pltpu.VMEM((length, depth), half_type),
            pltpu.VMEM((depth, 2 * LANES), half_type),
            pltpu.VMEM((kd, LANES), half_type),
            pltpu.VMEM((kd, LANES), half_type),
            pltpu.VMEM((length, LANES), full),
            pltpu.VMEM((length, LANES), full),
            pltpu.VMEM((n_seq, tok, span), full),
            pltpu.VMEM((2, length, LANES), half_type),
            pltpu.VMEM((length, LANES), half_type),
            pltpu.VMEM((length, LANES), half_type),
            pltpu.VMEM((length, LANES), half_type),
            pltpu.VMEM((n_seq, tok, LANES), half_type),
            dma((4,)),
            dma((n_x, PIECES)),
            dma((n_x, PIECES)),
            dma((PIECES,)),
            dma((n_seq, PIECES)),
            dma((3, n_dp, 2)),
            dma((n_dp, 2)),
            dma((n_seq,)),
            dma((n_seq,)),
        ],
        compiler_params=pltpu.CompilerParams(collective_id=0, has_side_effects=True),
    )(hidden_states, query_weight, key_weight, value_weight, doc_lengths)


def solution(mesh):
    placed = (P(("dp", "seq"), None), P("dp", None), P("dp", None), P("dp", None), P("dp", None))
    return jax.shard_map(
        shards, mesh=mesh, in_specs=placed, out_specs=P(("dp", "seq"), None), check_vma=False
    )
```

time: 121 us -> 32.6 us (0.27)
  blocking collectives: 73.4 us -> 0 us
  Pallas kernels: 0 us -> 30.9 us
  between operations: 13.6 us -> 0.01 us
  waiting for transfers between devices: 9.54 us -> 0 us
  matrix products: 8.37 us -> 0 us
  starting transfers between devices: 6.65 us -> 0 us
  other arithmetic: 4.16 us -> 0 us
  local copies, waits for them, and re-layouts: 3.63 us -> 1.57 us
  loops' own time: 1.41 us -> 0 us
    all_gather x2 -> x0, blocking collectives: 66.5 us -> none  [the longest x1 34.1 us: shards(): lax.all_gather(key_weight, 'dp', axis=0, tiled=True)]
    pallas_call x0 -> x1, Pallas kernels: none -> 30.9 us  [shards(): pl.pallas_call(functools.partial(kernel, n_dp, n_seq, docs), out_shape=ja...]
    all_to_all x2 -> x0, waiting for transfers between devices: 8.81 us -> none  [the longest x1 4.56 us: shards(): lax.all_to_all(repeated, 'seq', split_axis=1, concat_axis=0, tiled=True)]
    dot_general x7 -> x0, matrix products: 7.23 us -> none  [the longest x3 4.36 us: shards(): jnp.dot(normed, piece, preferred_element_type=jnp.float32)]
    all_to_all x1 -> x0, blocking collectives: 6.99 us -> none  [shards(): lax.all_to_all(mixed_heads, 'seq', split_axis=0, concat_axis=1, tiled=True)]
    all_to_all x2 -> x0, starting transfers between devices: 6.65 us -> none  [the longest x1 3.33 us: shards(): lax.all_to_all(repeated, 'seq', split_axis=1, concat_axis=0, tiled=True)]
    reduce_sum x2 -> x0, other arithmetic: 1.97 us -> none  [the longest x1 1.23 us: normalize(): jnp.mean(floats * floats, axis=-1, keepdims=True) + EPSILON]
    another operation x1 -> x0, loops' own time: 1.41 us -> none  [attend(): lax.map(one_block, jnp.arange(seq_length // block, dtype=jnp.int32))]
  transfers between devices with their start and end apart: 3 -> 0, of which waited for: 2 -> 0; matrix products, arithmetic and copies ran while one was open for 5% -> 0% of each run, Pallas kernels for 0% -> 0%
where the time goes in v1:
time: 32.6 us; the launch traced here: 32.5 us
  Pallas kernels  30.9 us (95%)
  local copies, waits for them, and re-layouts  1.57 us (5%)
    pallas_call x1, Pallas kernels, shards(): pl.pallas_call(functools.partial(kernel, n_dp, n_seq, docs), out_shape=ja...  30.9 us
    unnamed x1, local copies, waits for them, and re-layouts  1.57 us

profile of v1, /device:TPU:0, one launch (start us, length us, event | category | flops | bytes accessed | tf_op | source)
XLA Modules:
  0.0 32.5 jit_solution(14870508108646379710)
XLA Ops:
  0.0 30.9 %shard_map.55 = bf16[128,512]{1,0:T(8,128)(2,1)} custom-call(bf16[128,2048]{1,0:T(8,128)(2,1)} %h_ref.1, bf16[256,512]{1,0:T(8,128)(2,1)} %q_ref.1, bf16[256,128]{1,0:T(8,128)(2,1)} %k_ref.1, bf16[256,128]{1,0:T(8,128)(2,1)} %v_ref.1, s32[1,8]{1,0:T(1,128)} %len_ref.1), custom_call_target="tpu_custom_call" | custom-call | tf_op jit(solution)/shard_map/pallas_call | solution.py:350
  30.9 1.6 %copy.7 = bf16[128,512]{1,0:T(8,128)(2,1)} copy(bf16[128,512]{1,0:T(8,128)(2,1)} %shard_map.55) | data formatting | bytes 262144

commit v2 on v1

--- a/solution.py
+++ b/solution.py
@@ -21,7 +21,7 @@
 
 
 def kernel(n_dp, n_seq, docs, h_ref, q_ref, k_ref, v_ref, len_ref, out_ref,
-           hid, nrm, wbuf, kraw, vraw, cos_buf, sin_buf, bias, qs, ks, v0, v1, ctx,
+           lens, hid, nrm, wbuf, kraw, vraw, cos_buf, sin_buf, bias, qs, ks, v0, v1, ctx,
            loc_sem, hs_sem, hf_sem, hc_sem, hr_sem, ws_sem, wr_sem, os_sem, or_sem):
     dp = lax.axis_index("dp")
     me = lax.axis_index("seq")
@@ -51,6 +51,7 @@
         pltpu.make_async_copy(v_ref.at[:, pl.ds(kv_block, LANES)], vraw, loc_sem.at[1]),
         pltpu.make_async_copy(q_ref.at[:, q_cols], wbuf.at[own_rows(dp), pl.ds(0, LANES)], loc_sem.at[2]),
         pltpu.make_async_copy(h_ref, hid.at[me], loc_sem.at[3]),
+        pltpu.make_async_copy(len_ref, lens, loc_sem.at[4]),
     ]
     for copy in local:
         copy.start()
@@ -146,9 +147,10 @@
     send_own(1, start)
 
     half = HD // 2
-    ends = [len_ref[0, 0]]
+    local[4].wait()
+    ends = [lens[0, 0]]
     for j in range(1, docs):
-        ends.append(ends[-1] + len_ref[0, j])
+        ends.append(ends[-1] + lens[0, j])
     lane = lax.broadcasted_iota(jnp.int32, (tok, LANES), 1)
     row = lax.broadcasted_iota(jnp.int32, (tok, LANES), 0)
     freqs = jnp.exp((lane % half).astype(jnp.float32) * (-2.0 / HD) * math.log(THETA))
@@ -220,15 +222,23 @@
     for piece in range(PIECES):
         mate_h(mate, piece)
 
-    n_table = 0
-    for turn in range(max(PIECES, n_z - 1)):
-        if n_table < n_seq:
+    def far_mate(piece):
+        for step in range(1, n_x):
+            mate_h(((x + n_x - step) % n_x) * CORES + (1 - core), piece)
+
+    tables(0)
+    n_table = 1
+    turns = max(PIECES, n_z - 1)
+    for turn in range(turns):
+        if turn + 1 < n_z:
+            relay_w(turn + 1)
+        if turn < PIECES:
+            relay_h(turn)
+        if 0 < turn < PIECES:
+            far_mate(turn - 1)
+        if n_table < n_seq and turn + 1 < turns:
             tables(n_table)
             n_table += 1
-        if turn < PIECES:
-            relay_h(turn)
-        if turn + 1 < n_z:
-            relay_w(turn + 1)
     for block in range(n_table, n_seq):
         tables(block)
 
@@ -236,9 +246,7 @@
         shard = outer * INNER + (1 - y)
         for part in range(2):
             w_copy(shard, part, 2, across).wait_recv()
-    for piece in range(PIECES):
-        for step in range(1, n_x):
-            mate_h(((x + n_x - step) % n_x) * CORES + (1 - core), piece)
+    far_mate(PIECES - 1)
 
     strip = math.gcd(length, 512)
     lane_s = lax.broadcasted_iota(jnp.int32, (strip, LANES), 1)
@@ -349,10 +357,11 @@
     n_x = n_seq // CORES
     return pl.pallas_call(
         functools.partial(kernel, n_dp, n_seq, docs),
-        out_shape=jax.ShapeDtypeStruct((tok, query_weight.shape[1]), half_type),
-        in_specs=[any_spec] * 4 + [pl.BlockSpec(memory_space=pltpu.SMEM)],
+        out_shape=pltpu.VMEM((tok, query_weight.shape[1]), half_type),
+        in_specs=[any_spec] * 5,
         out_specs=pl.BlockSpec(memory_space=pltpu.VMEM),
         scratch_shapes=[
+            pltpu.SMEM((1, docs), jnp.int32),
             pltpu.VMEM((n_seq, tok, depth), half_type),
             pltpu.VMEM((length, depth), half_type),
             pltpu.VMEM((depth, 2 * LANES), half_type),
@@ -366,7 +375,7 @@
             pltpu.VMEM((length, LANES), half_type),
             pltpu.VMEM((length, LANES), half_type),
             pltpu.VMEM((n_seq, tok, LANES), half_type),
-            dma((4,)),
+            dma((5,)),
             dma((n_x, PIECES)),
             dma((n_x, PIECES)),
             dma((PIECES,)),

time: 32.6 us -> 28.8 us (0.88)
  Pallas kernels: 30.9 us -> 28 us
  local copies, waits for them, and re-layouts: 1.57 us -> 0.66 us
    pallas_call x1, Pallas kernels: 30.9 us -> 28 us  [shards(): pl.pallas_call(functools.partial(kernel, n_dp, n_seq, docs), out_shape=pl...]
    unnamed x1, local copies, waits for them, and re-layouts: 1.57 us -> 0.66 us
where the time goes in v2:
time: 28.8 us; the launch traced here: 28.7 us
  Pallas kernels  28 us (97%)
  local copies, waits for them, and re-layouts  0.66 us (2%)
    pallas_call x1, Pallas kernels, shards(): pl.pallas_call(functools.partial(kernel, n_dp, n_seq, docs), out_shape=pl...  28 us
    unnamed x1, local copies, waits for them, and re-layouts  0.66 us

profile of v2, /device:TPU:0, one launch (start us, length us, event | category | flops | bytes accessed | tf_op | source)
XLA Modules:
  0.0 28.7 jit_solution(4103786860903561749)
XLA Ops:
  0.0 28.0 %shard_map.55 = bf16[128,512]{1,0:T(8,128)(2,1)S(1)} custom-call(bf16[128,2048]{1,0:T(8,128)(2,1)} %h_ref.1, bf16[256,512]{1,0:T(8,128)(2,1)} %q_ref.1, bf16[256,128]{1,0:T(8,128)(2,1)} %k_ref.1, bf16[256,128]{1,0:T(8,128)(2,1)} %v_ref.1, s32[1,8]{1,0:T(1,128)} %len_ref.1), custom_call_target="tpu_custom_call" | custom-call | tf_op jit(solution)/shard_map/pallas_call | solution.py:358
  28.0 0.7 %copy.7 = bf16[128,512]{1,0:T(8,128)(2,1)} copy(bf16[128,512]{1,0:T(8,128)(2,1)S(1)} %shard_map.55) | data formatting | bytes 262144

commit v3 on v2

--- a/solution.py
+++ b/solution.py
@@ -13,7 +13,7 @@
 LANES = 128
 INNER = 2
 CORES = 2
-PIECES = 4
+PIECES = 8
 EPSILON = 1e-05
 THETA = 500000.0
 NEG_FILL = -1e30
@@ -228,10 +228,11 @@
 
     tables(0)
     n_table = 1
-    turns = max(PIECES, n_z - 1)
+    stride = max(1, PIECES // 4)
+    turns = max(PIECES, stride * (n_z - 1))
     for turn in range(turns):
-        if turn + 1 < n_z:
-            relay_w(turn + 1)
+        if turn % stride == 0 and turn // stride + 1 < n_z:
+            relay_w(turn // stride + 1)
         if turn < PIECES:
             relay_h(turn)
         if 0 < turn < PIECES:
@@ -246,14 +247,15 @@
         shard = outer * INNER + (1 - y)
         for part in range(2):
             w_copy(shard, part, 2, across).wait_recv()
-    far_mate(PIECES - 1)
-
-    strip = math.gcd(length, 512)
+
+    strip = CORES * tok
     lane_s = lax.broadcasted_iota(jnp.int32, (strip, LANES), 1)
     low_half = lane_s % HD < half
     low_head = lane_s < HD
-    for base in range(0, length, strip):
-        place = slice(base, base + strip)
+    for step in range(n_x):
+        if step == 1:
+            far_mate(PIECES - 1)
+        place = pl.ds(pl.multiple_of(((x + n_x - step) % n_x) * strip, strip), strip)
         lin = jnp.dot(nrm[place], wbuf[...], preferred_element_type=jnp.float32)
         cosine, sine = cos_buf[place], sin_buf[place]
 

time: 28.8 us -> 29.3 us (1.017)
  Pallas kernels: 28 us -> 28.5 us
    pallas_call x1, Pallas kernels: 28 us -> 28.5 us  [shards(): pl.pallas_call(functools.partial(kernel, n_dp, n_seq, docs), out_shape=pl...]
where the time goes in v3:
time: 29.3 us; the launch traced here: 29.1 us
  Pallas kernels  28.5 us (97%)
  local copies, waits for them, and re-layouts  0.66 us (2%)
    pallas_call x1, Pallas kernels, shards(): pl.pallas_call(functools.partial(kernel, n_dp, n_seq, docs), out_shape=pl...  28.5 us
    unnamed x1, local copies, waits for them, and re-layouts  0.66 us

profile of v3, /device:TPU:0, one launch (start us, length us, event | category | flops | bytes accessed | tf_op | source)
XLA Modules:
  0.0 29.1 jit_solution(9342614290684919)
XLA Ops:
  0.0 28.5 %shard_map.55 = bf16[128,512]{1,0:T(8,128)(2,1)S(1)} custom-call(bf16[128,2048]{1,0:T(8,128)(2,1)} %h_ref.1, bf16[256,512]{1,0:T(8,128)(2,1)} %q_ref.1, bf16[256,128]{1,0:T(8,128)(2,1)} %k_ref.1, bf16[256,128]{1,0:T(8,128)(2,1)} %v_ref.1, s32[1,8]{1,0:T(1,128)} %len_ref.1), custom_call_target="tpu_custom_call" | custom-call | tf_op jit(solution)/shard_map/pallas_call | solution.py:360
  28.5 0.7 %copy.7 = bf16[128,512]{1,0:T(8,128)(2,1)} copy(bf16[128,512]{1,0:T(8,128)(2,1)S(1)} %shard_map.55) | data formatting | bytes 262144

commit v4 on v2

--- a/solution.py
+++ b/solution.py
@@ -14,6 +14,7 @@
 INNER = 2
 CORES = 2
 PIECES = 4
+PARTS = 4
 EPSILON = 1e-05
 THETA = 500000.0
 NEG_FILL = -1e30
@@ -99,7 +100,8 @@
         return h_copy(hid.at[source, piece_rows(piece)], source, piece, hf_sem.at[step, piece], mate)
 
     def w_copy(shard, part, way, target, src=None):
-        place = wbuf.at[own_rows(shard), pl.ds(part * LANES, LANES)]
+        base = pl.multiple_of(shard * kd + (part % 2) * (kd // 2), kd // 2)
+        place = wbuf.at[pl.ds(base, kd // 2), pl.ds(part // 2 * LANES, LANES)]
         return pltpu.make_async_remote_copy(
             src_ref=place if src is None else src,
             dst_ref=place,
@@ -110,7 +112,8 @@
         )
 
     def w_own(part, way, target):
-        return w_copy(dp, part, way, target, q_ref.at[:, q_cols] if part == 0 else None)
+        src = q_ref.at[pl.ds((part % 2) * (kd // 2), kd // 2), q_cols] if part < 2 else None
+        return w_copy(dp, part, way, target, src)
 
     def send_own(part, act):
         @pl.when(has_left)
@@ -129,6 +132,7 @@
     for step in range(1, n_x):
         h_to_x(step, 0).start()
     send_own(0, start)
+    send_own(1, start)
     for piece in range(1, PIECES):
         for step in range(1, n_x):
             h_to_x(step, piece).start()
@@ -144,7 +148,8 @@
     second = jnp.where(kv_odd, vw, pltpu.roll(vw, HD, 1))
     wbuf[own_rows(dp), LANES:] = jnp.where(lane_k < HD, first, second).astype(wbuf.dtype)
     local[2].wait()
-    send_own(1, start)
+    send_own(2, start)
+    send_own(3, start)
 
     half = HD // 2
     local[4].wait()
@@ -189,7 +194,7 @@
             normalize(((x + n_x - step) % n_x) * CORES + core, piece)
 
     def relay_w(d):
-        for part in range(2):
+        for part in range(PARTS):
             @pl.when(z >= d)
             def _():
                 shard = dp - d * INNER
@@ -244,7 +249,7 @@
 
     for outer in range(n_z):
         shard = outer * INNER + (1 - y)
-        for part in range(2):
+        for part in range(PARTS):
             w_copy(shard, part, 2, across).wait_recv()
     far_mate(PIECES - 1)
 
@@ -324,7 +329,7 @@
         for step in range(1, n_x):
             h_to_x(step, piece).wait_send()
             h_forward(step, piece).wait_send()
-    for part in range(2):
+    for part in range(PARTS):
         send_own(part, wait_send)
         for d in range(1, n_z):
             @pl.when(z >= d)
@@ -380,8 +385,8 @@
             dma((n_x, PIECES)),
             dma((PIECES,)),
             dma((n_seq, PIECES)),
-            dma((3, n_dp, 2)),
-            dma((n_dp, 2)),
+            dma((3, n_dp, PARTS)),
+            dma((n_dp, PARTS)),
             dma((n_seq,)),
             dma((n_seq,)),
         ],

time: 28.8 us -> 28.1 us (0.976)
  Pallas kernels: 28 us -> 27.3 us
    pallas_call x1, Pallas kernels: 28 us -> 27.3 us  [shards(): pl.pallas_call(functools.partial(kernel, n_dp, n_seq, docs), out_shape=pl...]
where the time goes in v4:
time: 28.1 us; the launch traced here: 28 us
  Pallas kernels  27.3 us (97%)
  local copies, waits for them, and re-layouts  0.66 us (2%)
    pallas_call x1, Pallas kernels, shards(): pl.pallas_call(functools.partial(kernel, n_dp, n_seq, docs), out_shape=pl...  27.3 us
    unnamed x1, local copies, waits for them, and re-layouts  0.66 us

profile of v4, /device:TPU:0, one launch (start us, length us, event | category | flops | bytes accessed | tf_op | source)
XLA Modules:
  0.0 28.0 jit_solution(1975990728262421394)
XLA Ops:
  0.0 27.3 %shard_map.55 = bf16[128,512]{1,0:T(8,128)(2,1)S(1)} custom-call(bf16[128,2048]{1,0:T(8,128)(2,1)} %h_ref.1, bf16[256,512]{1,0:T(8,128)(2,1)} %q_ref.1, bf16[256,128]{1,0:T(8,128)(2,1)} %k_ref.1, bf16[256,128]{1,0:T(8,128)(2,1)} %v_ref.1, s32[1,8]{1,0:T(1,128)} %len_ref.1), custom_call_target="tpu_custom_call" | custom-call | tf_op jit(solution)/shard_map/pallas_call | solution.py:363
  27.3 0.7 %copy.7 = bf16[128,512]{1,0:T(8,128)(2,1)} copy(bf16[128,512]{1,0:T(8,128)(2,1)S(1)} %shard_map.55) | data formatting | bytes 262144
